TPU v7x, 256 devices: a whole 4x4x8 slice. The times are simulated.
256 devices in a mesh: comp: 2 (over x_lo), panel: 4 (over x_hi, core), col: 32 (over z, y).
Axes of the slice: x: 4 (x_hi: 2, x_lo: 2; x = x_hi * 2 + x_lo), y: 4, z: 8, core: 2. Of those that a mesh axis runs over, the one named last changes fastest.
Arguments:
- joint_tracer_field: float32 [2, 2, 4, 2048, 1024], P('comp', None, None, 'col', 'panel'), may hold values from -5 to 5
- courant_mixing_rates: float32 [2, 3, 4, 2048, 1024], P('comp', None, None, 'col', 'panel'), may hold values from -0.24 to 0.24, as said below
- oceanic_indicator: int32 [2, 2048, 1024], P('comp', 'col', 'panel'), may hold values 0 or 1
- glacial_indicator: int32 [2048, 1024], P('col', 'panel'), may hold values 0 or 1
- prior_oceanic_warmth: float32 [2048, 1024], P('col', 'panel'), may hold values from -4 to 4
- prior_glacial_cover: float32 [2048, 1024], P('col', 'panel'), may hold values from 0 to 0.8
- partner_devices: int32 [16384, 2], P(('panel', 'col')), may hold values from 0 to 127, all different within a row; in each aligned block of 128 rows (0 to 127, 128 to 255, ...) at most 4 rows name the same one
- receiving_tile_index: int32 [16384, 2], P(('panel', 'col')), may hold values from 0 to 127
- bank_tile_entry: int32 [16384, 2], P(('panel', 'col')), may hold values from 0 to 31
- conservative_overlay_factors: float32 [32, 128, 128], replicated, may hold values from 0.002 to 0.014
Outputs:
- new_state: float32 [2, 2, 4, 2048, 1024], P('comp', None, None, 'col', 'panel')
- surface: float32 [2, 2, 2048, 1024], P('comp', None, 'col', 'panel')
Inputs may be any that keep to these rules, and one draw needn't show every extreme that they name: `partner_devices`: each row names two different ocean devices, device p * 32 + q lying at index p of panel and q of col. Among the 128 rows of one device no ocean device is named more than 4 times, and in the rows of some devices one is named exactly 4 times. courant_mixing_rates[c, 0] and courant_mixing_rates[c, 1] lie in [-0.24, 0.24]; courant_mixing_rates[c, 2] lies in [0.01, 0.24].
All inputs are finite; a program needn't handle non-finite values. No bound on the sum of `oceanic_indicator` or of `glacial_indicator` on one device may be relied on, other than what follows from the above.
Results may differ from a plain program's by a relative error of at most 0.00013.
Values sent between devices are 32-bit elements; how exact they have to be, the bound alone decides.
A program may use at most 64 MiB of HBM per device.

v0:
```python
import jax
import jax.numpy as jnp
from jax import lax
from jax.sharding import PartitionSpec as P

TILE = 128
NSUB = 4
HIGHEST = lax.Precision.HIGHEST


def passed_along(value, axis, steps):
    count = lax.axis_size(axis)
    initial, last = (max(0, -steps), min(count, count - steps))
    return lax.ppermute(value, axis, [(source, source + steps) for source in range(initial, last)])


def from_behind(array, axis, by):
    count = lax.axis_size(axis)
    return lax.ppermute(array, axis, [(i, (i + by) % count) for i in range(count)])


def wide_halo(array, width):
    west = from_behind(array[..., -width:], "panel", 1)
    east = from_behind(array[..., :width], "panel", -1)
    array = jnp.concatenate([west, array, east], axis=-1)
    south = passed_along(array[..., -width:, :], "col", 1)
    north = passed_along(array[..., :width, :], "col", -1)
    return jnp.concatenate([south, array, north], axis=-2)


def vertical_mix(tracer, mixing):
    level_flux = mixing[:-1] * (tracer[:, 1:] - tracer[:, :-1])
    zero_level = jnp.zeros_like(tracer[:, :1])
    from_above = jnp.concatenate([level_flux, zero_level], axis=1)
    from_below = jnp.concatenate([zero_level, level_flux], axis=1)
    relaxation = jnp.concatenate(
        [jnp.zeros_like(tracer[:, :-1]), mixing[-1:] * tracer[:, -1:]], axis=1
    )
    return tracer + from_above - from_below - relaxation


def advect_mix(tracer, east_vel, north_vel, mixing):
    centre = tracer[..., 1:-1, 1:-1]
    vel_east = east_vel[:, 1:-1, 1:-1]
    vel_west = east_vel[:, 1:-1, :-2]
    vel_north = north_vel[:, 1:-1, 1:-1]
    vel_south = north_vel[:, :-2, 1:-1]
    flux_east = (
        jnp.maximum(vel_east, 0.0) * centre + jnp.minimum(vel_east, 0.0) * tracer[..., 1:-1, 2:]
    )
    flux_west = (
        jnp.maximum(vel_west, 0.0) * tracer[..., 1:-1, :-2] + jnp.minimum(vel_west, 0.0) * centre
    )
    flux_north = (
        jnp.maximum(vel_north, 0.0) * centre + jnp.minimum(vel_north, 0.0) * tracer[..., 2:, 1:-1]
    )
    flux_south = (
        jnp.maximum(vel_south, 0.0) * tracer[..., :-2, 1:-1] + jnp.minimum(vel_south, 0.0) * centre
    )
    advanced = centre - (flux_east - flux_west) - (flux_north - flux_south)
    return vertical_mix(advanced, mixing[:, 1:-1, 1:-1])


def to_tiles(field_grid):
    fcount, grid_rows, grid_cols = field_grid.shape
    blocks = field_grid.reshape(fcount, grid_rows, grid_cols // TILE, TILE)
    return blocks.transpose(1, 2, 0, 3).reshape(-1, fcount, TILE)


def from_tiles(tile_form, grid_rows, grid_cols):
    fcount = tile_form.shape[1]
    blocks = tile_form.reshape(grid_rows, grid_cols // TILE, fcount, TILE)
    return blocks.transpose(2, 0, 1, 3).reshape(fcount, grid_rows, grid_cols)


def bucket_places(partner_devices, owners, capacity):
    owner_list = partner_devices.reshape(-1)
    owner_hit = (owner_list[:, None] == jnp.arange(owners, dtype=jnp.int32)[None, :]).astype(
        jnp.int32
    )
    owner_rank = jnp.cumsum(owner_hit, axis=0) - owner_hit
    position = jnp.sum(owner_rank * owner_hit, axis=1)
    return owner_list * capacity + position


def advect(start, coeffs, grid_rows):
    fields = start.shape[0] * start.shape[1]
    both = jnp.concatenate(
        [start.reshape((fields,) + start.shape[2:]), coeffs.reshape((-1,) + coeffs.shape[2:])]
    )
    wide = wide_halo(both, NSUB)
    levels = coeffs.shape[1]
    tracer = wide[:fields].reshape(start.shape[:2] + wide.shape[1:])
    coeff_ext = wide[fields:].reshape((3, levels) + wide.shape[1:])
    rows_total = grid_rows * lax.axis_size("col")
    row_global = (
        lax.axis_index("col") * grid_rows + jnp.arange(grid_rows + 2 * NSUB, dtype=jnp.int32) - NSUB
    )
    row_open = ((row_global >= 0) & (row_global < rows_total - 1)).astype(jnp.float32)
    east_ext = coeff_ext[0]
    north_ext = coeff_ext[1] * row_open[None, :, None]
    mix_ext = coeff_ext[2]
    for step_index in range(NSUB):
        s = step_index
        e = east_ext.shape[1] - s
        w = east_ext.shape[2] - s
        tracer = advect_mix(
            tracer, east_ext[:, s:e, s:w], north_ext[:, s:e, s:w], mix_ext[:, s:e, s:w]
        )
    return tracer


def on_device(
    joint_tracer_field,
    courant_mixing_rates,
    oceanic_indicator,
    glacial_indicator,
    prior_oceanic_warmth,
    prior_glacial_cover,
    partner_devices,
    receiving_tile_index,
    bank_tile_entry,
    conservative_overlay_factors,
):
    owners = lax.axis_size("panel") * lax.axis_size("col")
    tile_count = partner_devices.shape[0]
    capacity = max(2, 4 * tile_count // owners)
    slots = owners * capacity
    nbank = conservative_overlay_factors.shape[0]
    on_atmos = lax.axis_index("comp") == 0
    device_tracer_share = joint_tracer_field[0]
    coeffs = courant_mixing_rates[0]
    grid_rows = coeffs.shape[2]
    grid_cols = coeffs.shape[3]
    sea_here = oceanic_indicator[0].astype(jnp.float32)
    wind_east = coeffs[0, 0]
    wind_north = coeffs[1, 0]
    airflow_speed = jnp.sqrt(wind_east * wind_east + wind_north * wind_north + 0.01)
    unfrozen_share = sea_here * (1.0 - prior_glacial_cover)
    thermal_exchange_rate = (
        2.0 * airflow_speed * (prior_oceanic_warmth - device_tracer_share[0, 0]) * unfrozen_share
    )
    evaporation_rate = (
        2.0
        * airflow_speed
        * (jnp.exp(0.1 * prior_oceanic_warmth) - device_tracer_share[1, 0])
        * unfrozen_share
    )
    heated = device_tracer_share.at[0, 0].add(thermal_exchange_rate).at[1, 0].add(evaporation_rate)
    start = jnp.where(on_atmos, heated, device_tracer_share)
    surface_flux = jnp.stack([thermal_exchange_rate, evaporation_rate])
    flux_rows = passed_along(to_tiles(surface_flux), "comp", 1).reshape(tile_count * 2, TILE)
    pairs = tile_count * 2
    bucket_place = bucket_places(partner_devices, owners, capacity)
    place_match = bucket_place[None, :] == jnp.arange(slots, dtype=jnp.int32)[:, None]
    slot_used = jnp.any(place_match, axis=1)
    slot_pair = jnp.sum(
        jnp.where(place_match, jnp.arange(pairs, dtype=jnp.int32)[None, :], 0), axis=1
    )
    slot_tile = slot_pair // 2
    slot_bank = jnp.sum(jnp.where(place_match, bank_tile_entry.reshape(-1)[None, :], 0), axis=1)
    by_bank = jnp.einsum(
        "bji,ri->brj", conservative_overlay_factors, flux_rows, precision=lax.Precision.HIGH
    ).reshape(nbank * pairs, TILE)
    f_ids = jnp.arange(2, dtype=jnp.int32)[None, :]
    slot_rows = (slot_bank * pairs + slot_tile * 2)[:, None] + f_ids
    picked = by_bank[slot_rows.reshape(-1)].reshape(slots, 2, TILE)
    buffer = jnp.where(slot_used[:, None, None], picked, 0.0).reshape(owners, capacity * 2, TILE)
    received = lax.all_to_all(buffer, ("panel", "col"), 0, 0, tiled=True).reshape(slots * 2, TILE)
    me = lax.axis_index("panel") * lax.axis_size("col") + lax.axis_index("col")
    own_routes = jnp.concatenate([partner_devices.T, receiving_tile_index.T], axis=0)
    owner_ids = jnp.arange(owners, dtype=jnp.int32)[:, None, None]
    routes = lax.psum(
        jnp.where(owner_ids == me, own_routes[None].astype(jnp.float32), 0.0), ("panel", "col")
    ).astype(jnp.int32)
    mine = [(routes[:, k] == me).astype(jnp.int32) for k in range(2)]
    per_tile = mine[0] + mine[1]
    before = jnp.cumsum(per_tile, axis=1) - per_tile
    rank = [before, before + mine[0]]
    recv_slots = jnp.stack(
        [
            sum((jnp.sum(mine[k] * (rank[k] == c) * routes[:, 2 + k], axis=1) for k in range(2)))
            for c in range(capacity)
        ],
        axis=1,
    ).reshape(-1)
    row_ids = lax.broadcasted_iota(jnp.int32, (pairs, slots * 2), 0)
    col_ids = lax.broadcasted_iota(jnp.int32, (pairs, slots * 2), 1)
    recv_rep = jnp.broadcast_to(recv_slots[:, None], (slots, 2)).reshape(-1)
    slot_hit2 = ((recv_rep[None, :] == row_ids // 2) & (col_ids % 2 == row_ids % 2)).astype(
        jnp.float32
    )
    summed = jnp.dot(slot_hit2, received, precision=HIGHEST)
    forcing = from_tiles(summed.reshape(tile_count, 2, TILE), grid_rows, grid_cols)
    tracer = advect(start, coeffs, grid_rows)
    forced = (
        tracer.at[0, 0]
        .add(-(0.5 * sea_here * forcing[0]))
        .at[1, 0]
        .add(0.5 * sea_here * forcing[1])
    )
    new_here = jnp.where(on_atmos, tracer, forced)
    sea_temp = new_here[0, 0]
    ice_cover = (
        glacial_indicator.astype(jnp.float32) * sea_here * jnp.clip(0.5 - sea_temp, 0.0, 1.0)
    )
    ocean_surface = jnp.stack([sea_temp, ice_cover])
    ocean_tiles = to_tiles(ocean_surface).reshape(pairs, TILE)
    reply = jnp.dot(slot_hit2.T, ocean_tiles, precision=HIGHEST).reshape(owners, capacity * 2, TILE)
    returned = lax.all_to_all(reply, ("panel", "col"), 0, 0, tiled=True).reshape(slots * 2, TILE)
    place_rep = jnp.broadcast_to(bucket_place[:, None], (pairs, 2)).reshape(-1)
    p_rows = lax.broadcasted_iota(jnp.int32, (pairs * 2, slots * 2), 0)
    p_cols = lax.broadcasted_iota(jnp.int32, (pairs * 2, slots * 2), 1)
    place_hit2 = ((place_rep[:, None] == p_cols // 2) & (p_cols % 2 == p_rows % 2)).astype(
        jnp.float32
    )
    values = jnp.dot(place_hit2, returned, precision=HIGHEST)
    by_bank_back = jnp.einsum(
        "rj,bji->bri", values, conservative_overlay_factors, precision=lax.Precision.HIGH
    ).reshape(nbank * pairs * 2, TILE)
    tile_ids = jnp.arange(tile_count, dtype=jnp.int32)[:, None]
    pair_rows = (bank_tile_entry * tile_count + tile_ids) * 4 + jnp.arange(2, dtype=jnp.int32)[
        None, :
    ] * 2
    back_rows = pair_rows[:, :, None] + f_ids[:, None, :]
    numerator = jnp.sum(by_bank_back[back_rows.reshape(-1)].reshape(tile_count, 2, 2, TILE), axis=1)
    column_sums = jnp.sum(conservative_overlay_factors, axis=1)
    bank_ids = jnp.arange(nbank, dtype=jnp.int32)[None, :]
    bank_count = (bank_tile_entry[:, :1] == bank_ids).astype(jnp.float32) + (
        bank_tile_entry[:, 1:] == bank_ids
    ).astype(jnp.float32)
    denominator = jnp.dot(bank_count, column_sums, precision=HIGHEST)
    remap_back = numerator / denominator[:, None, :]
    remapped = passed_along(from_tiles(remap_back, grid_rows, grid_cols), "comp", -1)
    surface_here = jnp.where(on_atmos, remapped, ocean_surface)
    return (new_here[None], surface_here[None])


def solution(mesh):
    return jax.shard_map(
        on_device,
        mesh=mesh,
        in_specs=(
            P("comp", None, None, "col", "panel"),
            P("comp", None, None, "col", "panel"),
            P("comp", "col", "panel"),
            P("col", "panel"),
            P("col", "panel"),
            P("col", "panel"),
            P(("panel", "col"), None),
            P(("panel", "col"), None),
            P(("panel", "col"), None),
            P(),
        ),
        out_specs=(P("comp", None, None, "col", "panel"), P("comp", None, "col", "panel")),
        check_vma=False,
    )
```

profile of v0, /device:TPU:1, one launch (start us, length us, event | category | flops | bytes accessed | tf_op | source)
XLA Modules:
  0.0 1241.6 jit_solution(11290199410697722666)
XLA Ops:
  7.2 2.1 copy.125
  10.3 1.5 bitcast_dynamic-update-slice_fusion
  11.8 1.7 fusion.81
  16.1 2.0 copy.93
  18.1 3.2 collective-permute-start.1
  21.3 2.0 copy.92
  26.5 3.5 collective-permute-start.4
  48.8 1.9 copy.95
  50.7 1.9 copy.94
  52.6 1.3 pad_maximum_fusion.8
  55.3 4.2 collective-permute-start.2
  59.7 1.5 collective-permute-done.3
  74.5 5.1 fusion.135
  79.6 5.0 gather_fusion
  85.6 18.1 %all-to-all-start = ((f32[128,8,128]{2,1,0:T(8,128)}), f32[128,8,128]{2,1,0:T(8,128)}, u32[]{:S(2)}, u32[]{:S(2)}) async-start(f32[128,8,128]{2,1,0:T(8,128)} %bitcast_select_fusion), calls=%async_computation | async-start | bytes 1048576 | tf_op jit(solution)/shard_map/all_to_all | solution.py:169
  103.7 1047.6 %all-reduce.14.cloned.1.call-done = f32[128,4,128]{0,2,1:T(8,128)} async-done(((f32[128,4,128]{0,2,1:T(8,128)}), f32[128,4,128]{0,2,1:T(8,128)}) %all-reduce.14.cloned.1.call-update) | async-done | bytes 262160 | tf_op jit(solution)/shard_map/psum | solution.py:173
  1153.3 1.5 fusion.15
  1154.8 1.9 convolution_bitcast_fusion
  1158.1 1.5 fusion.17
  1159.6 36.4 %all-to-all-start.1 = ((f32[128,8,128]{2,1,0:T(8,128)}), f32[128,8,128]{2,1,0:T(8,128)S(1)}, u32[]{:S(2)}, u32[]{:S(2)}) async-start(f32[128,8,128]{2,1,0:T(8,128)} %fusion.17), calls=%async_computation.1 | async-start | bytes 1048576 | tf_op jit(solution)/shard_map/all_to_all | solution.py:210
  1197.5 18.6 %all-to-all-done.1 = f32[128,8,128]{2,1,0:T(8,128)S(1)} async-done(((f32[128,8,128]{2,1,0:T(8,128)}), f32[128,8,128]{2,1,0:T(8,128)S(1)}, u32[]{:S(2)}, u32[]{:S(2)}) %all-to-all-start.1) | async-done | bytes 524320 | tf_op jit(solution)/shard_map/all_to_all | solution.py:210
  1217.3 5.6 fusion.136
  1222.9 4.4 gather_fusion.1
  1229.1 5.0 collective-permute-done.5
  (202 shorter events, 49.2 us)
Async XLA Ops:
  7.2 67.3 %copy-start = (f32[32,128,128]{2,1,0:T(8,128)S(1)}, f32[32,128,128]{2,1,0:T(8,128)}, u32[]{:S(2)}) copy-start(f32[32,128,128]{2,1,0:T(8,128)} %param.27) | copy-start | bytes 6291460
  7.2 1144.2 %all-reduce.14.cloned.1.call-start = ((), (), s32[]{:S(2)}) async-start(), calls=%async_computation.2 | async-start | bytes 524288 | tf_op jit(solution)/shard_map/psum | solution.py:173
  14.8 15.3 %copy-start.22 = (s32[128,2]{0,1:T(2,128)S(1)}, s32[128,2]{0,1:T(2,128)}, u32[]{:S(2)}) copy-start(s32[128,2]{0,1:T(2,128)} %param.24) | copy-start | bytes 3076
  18.1 25.2 %copy-start.15 = (s32[128,2]{0,1:T(2,128)S(1)}, s32[128,2]{0,1:T(2,128)}, u32[]{:S(2)}) copy-start(s32[128,2]{0,1:T(2,128)} %param.26) | copy-start | bytes 3076
  18.1 30.7 %collective-permute-start.1 = (f32[20,64,4]{1,2,0:T(4,128)}, f32[20,64,4]{1,2,0:T(4,128)}, u32[]{:S(2)}, u32[]{:S(2)}) collective-permute-start(f32[20,64,4]{1,2,0:T(4,128)} %copy.93), channel_id=1, source_target_pairs={{0,96},{32,0},{64,32},{96,64},{1,97},{33,1},{65,33},{97,65},{2,98}... | collective-permute-start | bytes 61448 | tf_op jit(solution)/shard_map/ppermute | solution.py:19
  23.2 27.5 %collective-permute-start = (f32[20,64,4]{1,2,0:T(4,128)}, f32[20,64,4]{1,2,0:T(4,128)}, u32[]{:S(2)}, u32[]{:S(2)}) collective-permute-start(f32[20,64,4]{1,2,0:T(4,128)} %copy.92), channel_id=1, source_target_pairs={{0,32},{32,64},{64,96},{96,0},{1,33},{33,65},{65,97},{97,1},{2,34}... | collective-permute-start | bytes 61448 | tf_op jit(solution)/shard_map/ppermute | solution.py:19
  26.5 47.9 %collective-permute-start.4 = (f32[128,2,128]{2,1,0:T(2,128)}, f32[128,2,128]{2,1,0:T(2,128)}, u32[]{:S(2)}, u32[]{:S(2)}) collective-permute-start(f32[128,2,128]{2,1,0:T(2,128)} %bitcast.33), channel_id=1, source_target_pairs={{0,128},{1,129},{2,130},{3,131},{4,132},{5,133},{6,134},{7,135},{8... | collective-permute-start | bytes 393224 | tf_op jit(solution)/shard_map/ppermute | solution.py:14
  54.0 7.1 collective-permute-start.3
  55.3 7.1 collective-permute-start.2
  84.6 1068.7 %copy-start.18 = (s32[256]{0:T(256)S(1)}, s32[256]{0:T(256)}, u32[]{:S(2)}) copy-start(s32[256]{0:T(256)} %get-tuple-element.138) | copy-start | bytes 3076
  84.6 1068.7 %copy-start.19 = (s32[256]{0:T(256)S(1)}, s32[256]{0:T(256)}, u32[]{:S(2)}) copy-start(s32[256]{0:T(256)} %get-tuple-element.139) | copy-start | bytes 3076
  84.6 1068.7 %copy-start.20 = (s32[256]{0:T(256)S(1)}, s32[256]{0:T(256)}, u32[]{:S(2)}) copy-start(s32[256]{0:T(256)} %get-tuple-element.140) | copy-start | bytes 3076
  84.6 1068.7 %copy-start.21 = (s32[256]{0:T(256)S(1)}, s32[256]{0:T(256)}, u32[]{:S(2)}) copy-start(s32[256]{0:T(256)} %get-tuple-element.141) | copy-start | bytes 3076
  84.6 1070.2 %copy-start.23 = (s32[1024]{0:T(1024)S(1)}, s32[1024]{0:T(1024)}, u32[]{:S(2)}) copy-start(s32[1024]{0:T(1024)} %get-tuple-element.128) | copy-start | bytes 12292
  84.6 1070.2 %copy-start.25 = (s32[1024]{0:T(1024)S(1)}, s32[1024]{0:T(1024)}, u32[]{:S(2)}) copy-start(s32[1024]{0:T(1024)} %get-tuple-element.129) | copy-start | bytes 12292
  84.6 1070.2 %copy-start.27 = (s32[64,2,2]{0,2,1:T(2,128)S(1)}, s32[64,2,2]{0,2,1:T(2,128)}, u32[]{:S(2)}) copy-start(s32[64,2,2]{0,2,1:T(2,128)} %get-tuple-element.134) | copy-start | bytes 3076
  85.6 1069.2 %all-to-all-start = ((f32[128,8,128]{2,1,0:T(8,128)}), f32[128,8,128]{2,1,0:T(8,128)}, u32[]{:S(2)}, u32[]{:S(2)}) async-start(f32[128,8,128]{2,1,0:T(8,128)} %bitcast_select_fusion), calls=%async_computation | async-start | bytes 1048576 | tf_op jit(solution)/shard_map/all_to_all | solution.py:169
  1156.9 39.1 %copy-start.17 = (s32[256]{0:T(256)S(1)}, s32[256]{0:T(256)}, u32[]{:S(2)}) copy-start(s32[256]{0:T(256)} %copy-done.16) | copy-start | bytes 3076
  1157.0 39.2 %copy-start.12 = (s32[128,2,2]{2,1,0:T(2,128)S(1)}, s32[128,2,2]{2,1,0:T(2,128)}, u32[]{:S(2)}) copy-start(s32[128,2,2]{2,1,0:T(2,128)} %iota_add_fusion.1) | copy-start | bytes 6148
  1158.1 58.0 %copy-start.24 = (s32[1024]{0:T(1024)S(1)}, s32[1024]{0:T(1024)}, u32[]{:S(2)}) copy-start(s32[1024]{0:T(1024)} %get-tuple-element.128) | copy-start | bytes 12292
  1158.1 58.0 %copy-start.26 = (s32[1024]{0:T(1024)S(1)}, s32[1024]{0:T(1024)}, u32[]{:S(2)}) copy-start(s32[1024]{0:T(1024)} %get-tuple-element.129) | copy-start | bytes 12292
  1158.1 58.0 %copy-start.29 = (pred[1024]{0:T(1024)(128)(4,1)S(1)}, pred[1024]{0:T(1024)(128)(4,1)}, u32[]{:S(2)}) copy-start(pred[1024]{0:T(1024)(128)(4,1)} %fusion.121) | copy-start | bytes 3076
  1159.6 56.4 %all-to-all-start.1 = ((f32[128,8,128]{2,1,0:T(8,128)}), f32[128,8,128]{2,1,0:T(8,128)S(1)}, u32[]{:S(2)}, u32[]{:S(2)}) async-start(f32[128,8,128]{2,1,0:T(8,128)} %fusion.17), calls=%async_computation.1 | async-start | bytes 1048576 | tf_op jit(solution)/shard_map/all_to_all | solution.py:210
  1227.8 6.3 collective-permute-start.5
  (15 other events, 67.5 us)
Sparse Core Ops, SparseCore 0:
  31.1 1120.2 all-reduce.13
where the time goes:
time: 1240 us
  waiting for transfers between devices  1070 us (86%)
  starting transfers between devices  69 us (6%)
  other arithmetic  38.4 us (3%)
  local copies, waits for them, and re-layouts  29.6 us (2%)
  matrix products  15.6 us (1%)
  between operations  15 us (1%)
    psum x1, waiting for transfers between devices, on_device(): lax.psum(jnp.where(owner_ids == me, own_routes[None].astype(jnp.float32),...  1050 us
    all_to_all x1, starting transfers between devices, on_device(): lax.all_to_all(reply, ('panel', 'col'), 0, 0, tiled=True)  36.4 us
  transfers between devices with their start and end apart: 9, of which 5 were waited for; matrix products, arithmetic and copies ran while one was open for 4% of the time, Pallas kernels for 0%

commit v1 on v0

--- a/solution.py
+++ b/solution.py
@@ -170,8 +170,12 @@
     me = lax.axis_index("panel") * lax.axis_size("col") + lax.axis_index("col")
     own_routes = jnp.concatenate([partner_devices.T, receiving_tile_index.T], axis=0)
     owner_ids = jnp.arange(owners, dtype=jnp.int32)[:, None, None]
-    routes = lax.psum(
-        jnp.where(owner_ids == me, own_routes[None].astype(jnp.float32), 0.0), ("panel", "col")
+
+    def group_body(shard_in):
+        return jnp.sum(lax.all_gather(shard_in, ("panel", "col")), axis=0)
+
+    routes = group_body(
+        jnp.where(owner_ids == me, own_routes[None].astype(jnp.float32), 0.0)
     ).astype(jnp.int32)
     mine = [(routes[:, k] == me).astype(jnp.int32) for k in range(2)]
     per_tile = mine[0] + mine[1]

time: 1240 us -> 312 us (0.25)
  waiting for transfers between devices: 1070 us -> 158 us
  starting transfers between devices: 69 us -> 41.6 us
    psum x1 -> x0, waiting for transfers between devices: 1050 us -> none  [on_device(): lax.psum(jnp.where(owner_ids == me, own_routes[None].astype(jnp.float32),...]
    all_gather x0 -> x1, waiting for transfers between devices: none -> 130 us  [group_body(): return jnp.sum(lax.all_gather(shard_in, ('panel', 'col')), axis=0)]
    all_to_all x1, starting transfers between devices: 36.4 us -> 8.42 us  [on_device(): lax.all_to_all(reply, ('panel', 'col'), 0, 0, tiled=True)]
  transfers between devices with their start and end apart: 9 -> 9, of which waited for: 5 -> 5; matrix products, arithmetic and copies ran while one was open for 4% -> 24% of each run, Pallas kernels for 0% -> 0%
where the time goes in v1:
time: 312 us; the launch traced here: 311 us
  waiting for transfers between devices  158 us (51%)
  other arithmetic  50.8 us (16%)
  starting transfers between devices  41.6 us (13%)
  local copies, waits for them, and re-layouts  30 us (10%)
  matrix products  15.6 us (5%)
  between operations  15.2 us (5%)
    all_gather x1, waiting for transfers between devices, group_body(): return jnp.sum(lax.all_gather(shard_in, ('panel', 'col')), axis=0)  130 us
    all_to_all x1, starting transfers between devices, on_device(): lax.all_to_all(buffer, ('panel', 'col'), 0, 0, tiled=True)  19.3 us
    all_to_all x1, waiting for transfers between devices, on_device(): lax.all_to_all(reply, ('panel', 'col'), 0, 0, tiled=True)  18.6 us
    reduce_sum x1, other arithmetic, group_body(): return jnp.sum(lax.all_gather(shard_in, ('panel', 'col')), axis=0)  12 us
    ppermute x4, starting transfers between devices, passed_along(): lax.ppermute(value, axis, [(source, source + steps) for source in range(i...  10.6 us
    ppermute x4, waiting for transfers between devices, passed_along(): lax.ppermute(value, axis, [(source, source + steps) for source in range(i...  8.96 us
    all_to_all x1, starting transfers between devices, on_device(): lax.all_to_all(reply, ('panel', 'col'), 0, 0, tiled=True)  8.42 us
  transfers between devices with their start and end apart: 9, of which 5 were waited for; matrix products, arithmetic and copies ran while one was open for 24% of the time, Pallas kernels for 0%

profile of v1, /device:TPU:1, one launch (start us, length us, event | category | flops | bytes accessed | tf_op | source)
XLA Modules:
  0.0 311.0 jit_solution(2105529935306060497)
XLA Ops:
  15.3 4.6 %collective-permute-start.4 = (f32[128,2,128]{2,1,0:T(2,128)}, f32[128,2,128]{2,1,0:T(2,128)}, u32[]{:S(2)}, u32[]{:S(2)}) collective-permute-start(f32[128,2,128]{2,1,0:T(2,128)} %bitcast.33), channel_id=1, source_target_pairs={{0,128},{1,129},{2,130},{3,131},{4,132},{5,133},{6,134},{7,135},{8... | collective-permute-start | bytes 393224 | tf_op jit(solution)/shard_map/ppermute | solution.py:14
  22.5 2.0 copy.119
  24.5 3.3 %collective-permute-start = (f32[20,64,4]{1,2,0:T(4,128)}, f32[20,64,4]{1,2,0:T(4,128)}, u32[]{:S(2)}, u32[]{:S(2)}) collective-permute-start(f32[20,64,4]{1,2,0:T(4,128)} %copy.119), channel_id=1, source_target_pairs={{0,32},{32,64},{64,96},{96,0},{1,33},{33,65},{65,97},{97,1},{2,34}... | collective-permute-start | bytes 61448 | tf_op jit(solution)/shard_map/ppermute | solution.py:19
  27.8 2.0 copy.120
  32.8 1.5 broadcast_in_dim.81
  47.1 1.9 copy.121
  49.0 1.9 copy.122
  50.9 1.3 pad_maximum_fusion.8
  52.2 3.2 %collective-permute-start.2 = (f32[20,4,264]{2,1,0:T(4,128)S(1)}, f32[20,4,264]{2,1,0:T(4,128)S(1)}, u32[]{:S(2)}, u32[]{:S(2)}) collective-permute-start(f32[20,4,264]{2,1,0:T(4,128)S(1)} %get-tuple-element.71), channel_id=1, source_target_pairs={{0,1},{1,2},{2,3},{3,4},{4,5},{5,6},{6,7},{7,8},{8,9},{9,10},{10,1... | collective-permute-start | bytes 253448 | tf_op jit(solution)/shard_map/ppermute | solution.py:14
  55.4 1.5 collective-permute-start.3
  57.3 3.8 %collective-permute-done.3 = f32[20,4,264]{2,1,0:T(4,128)S(1)} collective-permute-done((f32[20,4,264]{2,1,0:T(4,128)S(1)}, f32[20,4,264]{2,1,0:T(4,128)S(1)}, u32[]{:S(2)}, u32[]{:S(2)}) %collective-permute-start.3) | collective-permute-done | bytes 84512 | tf_op jit(solution)/shard_map/ppermute | solution.py:14
  74.2 5.0 %fusion.135 = f32[256,32,128]{2,0,1:T(8,128)} fusion(f32[256,128,1]{1,0,2:T(8,128)} %bitcast.35, f32[32,128,128]{2,1,0:T(8,128)S(1)} %copy-done), kind=kOutput, calls=%fused_computation.307 | convolution fusion | flops 805306368 | bytes 6422528 | tf_op jit(solution)/shard_map/bji,ri->brj/dot_general | solution.py:162
  79.2 5.0 %gather_fusion = f32[1024,128]{1,0:T(8,128)S(1)} fusion(f32[8192,128]{1,0:T(8,128)} %bitcast.285, s32[1024]{0:T(1024)S(1)} %broadcast_clamp_fusion), kind=kCustom, calls=%fused_computation | custom fusion | bytes 1052672 | tf_op jit(solution)/shard_map/gather | solution.py:167
  85.2 19.3 %all-to-all-start = ((f32[128,8,128]{2,1,0:T(8,128)}), f32[128,8,128]{2,1,0:T(8,128)}, u32[]{:S(2)}, u32[]{:S(2)}) async-start(f32[128,8,128]{2,1,0:T(8,128)} %bitcast_select_fusion), calls=%async_computation | async-start | bytes 1048576 | tf_op jit(solution)/shard_map/all_to_all | solution.py:169
  104.6 2.4 pad_subtract_fusion.3
  107.0 130.3 %all-gather.2.cloned.1.call-done = f32[128,128,4,128]{3,1,2,0:T(8,128)} async-done(((f32[1,128,4,128]{3,1,2,0:T(8,128)}), f32[128,128,4,128]{3,1,2,0:T(8,128)}) %all-gather.2.cloned.1.call-update) | async-done | bytes 33554448 | tf_op jit(solution)/shard_map/all_gather | solution.py:175
  237.3 12.0 %reduce_sum.128 = f32[128,4,128]{2,0,1:T(8,128)S(1)} reduce(f32[128,128,4,128]{3,1,2,0:T(8,128)} %all-gather.2.cloned.1.call-done, f32[]{:T(128)} %constant.263.clone.1), dimensions={0}, to_apply=%region_0.0 | reduce | flops 8323072 | bytes 33816580 | tf_op jit(solution)/shard_map/reduce_sum | solution.py:175
  250.4 1.9 convolution_bitcast_fusion
  255.4 1.5 fusion.17
  257.0 8.4 %all-to-all-start.1 = ((f32[128,8,128]{2,1,0:T(8,128)}), f32[128,8,128]{2,1,0:T(8,128)S(1)}, u32[]{:S(2)}, u32[]{:S(2)}) async-start(f32[128,8,128]{2,1,0:T(8,128)} %fusion.17), calls=%async_computation.1 | async-start | bytes 1048576 | tf_op jit(solution)/shard_map/all_to_all | solution.py:214
  266.9 18.6 %all-to-all-done.1 = f32[128,8,128]{2,1,0:T(8,128)S(1)} async-done(((f32[128,8,128]{2,1,0:T(8,128)}), f32[128,8,128]{2,1,0:T(8,128)S(1)}, u32[]{:S(2)}, u32[]{:S(2)}) %all-to-all-start.1) | async-done | bytes 524320 | tf_op jit(solution)/shard_map/all_to_all | solution.py:214
  286.7 5.6 %fusion.136 = f32[512,32,128]{2,0,1:T(8,128)} fusion(f32[512,128,1]{1,0,2:T(8,128)S(1)} %fusion.3, f32[32,128,128]{2,1,0:T(8,128)S(1)} %copy-done), kind=kOutput, calls=%fused_computation.308 | convolution fusion | flops 1610612736 | bytes 10747904 | tf_op jit(solution)/shard_map/rj,bji->bri/dot_general | solution.py:222
  292.3 4.4 %gather_fusion.1 = f32[512,128]{1,0:T(8,128)S(1)} fusion(f32[16384,128]{1,0:T(8,128)} %bitcast.286, s32[1024]{0:T(1024)S(1)} %pad_clamp_fusion), kind=kCustom, calls=%fused_computation.1 | custom fusion | bytes 526336 | tf_op jit(solution)/shard_map/gather | solution.py:230
  298.5 5.0 %collective-permute-done.5 = f32[2,64,256]{2,1,0:T(8,128)S(1)} collective-permute-done((f32[2,64,256]{2,1,0:T(8,128)S(1)}, f32[2,64,256]{2,1,0:T(8,128)S(1)}, u32[]{:S(2)}, u32[]{:S(2)}) %collective-permute-start.5) | collective-permute-done | bytes 131104 | tf_op jit(solution)/shard_map/ppermute | solution.py:14
  (216 shorter events, 49.4 us)
Async XLA Ops:
  7.2 67.0 %copy-start = (f32[32,128,128]{2,1,0:T(8,128)S(1)}, f32[32,128,128]{2,1,0:T(8,128)}, u32[]{:S(2)}) copy-start(f32[32,128,128]{2,1,0:T(8,128)} %param.27) | copy-start | bytes 6291460
  7.2 5.4 %copy-start.1 = (f32[1,3,4,64,256]{4,3,2,1,0:T(8,128)S(1)}, f32[1,3,4,64,256]{4,3,2,1,0:T(8,128)}, u32[]{:S(2)}) copy-start(f32[1,3,4,64,256]{4,3,2,1,0:T(8,128)} %param.19) | copy-start | bytes 2359300
  7.2 5.4 %copy-start.16 = (s32[1,64,256]{2,1,0:T(8,128)S(1)}, s32[1,64,256]{2,1,0:T(8,128)}, u32[]{:S(2)}) copy-start(s32[1,64,256]{2,1,0:T(8,128)} %param.20) | copy-start | bytes 196612
  7.2 230.1 %all-gather.2.cloned.1.call-start = ((), (), s32[]{:S(2)}) async-start(), calls=%async_computation.2 | async-start | bytes 33816576 | tf_op jit(solution)/shard_map/all_gather | solution.py:175
  13.6 6.4 %copy-start.7 = (f32[2,4,64,256]{3,2,1,0:T(8,128)}, f32[2,4,64,256]{3,2,1,0:T(8,128)S(1)}, u32[]{:S(2)}) copy-start(f32[2,4,64,256]{3,2,1,0:T(8,128)S(1)} %get-tuple-element.69) | copy-start | bytes 1572868
  15.3 58.8 %collective-permute-start.4 = (f32[128,2,128]{2,1,0:T(2,128)}, f32[128,2,128]{2,1,0:T(2,128)}, u32[]{:S(2)}, u32[]{:S(2)}) collective-permute-start(f32[128,2,128]{2,1,0:T(2,128)} %bitcast.33), channel_id=1, source_target_pairs={{0,128},{1,129},{2,130},{3,131},{4,132},{5,133},{6,134},{7,135},{8... | collective-permute-start | bytes 393224 | tf_op jit(solution)/shard_map/ppermute | solution.py:14
  21.2 8.5 %copy-start.29 = (s32[128,2]{0,1:T(2,128)S(1)}, s32[128,2]{0,1:T(2,128)}, u32[]{:S(2)}) copy-start(s32[128,2]{0,1:T(2,128)} %param.24) | copy-start | bytes 3076
  21.2 10.8 %copy-start.22 = (s32[128,2]{0,1:T(2,128)S(1)}, s32[128,2]{0,1:T(2,128)}, u32[]{:S(2)}) copy-start(s32[128,2]{0,1:T(2,128)} %param.26) | copy-start | bytes 3076
  24.5 22.6 %collective-permute-start = (f32[20,64,4]{1,2,0:T(4,128)}, f32[20,64,4]{1,2,0:T(4,128)}, u32[]{:S(2)}, u32[]{:S(2)}) collective-permute-start(f32[20,64,4]{1,2,0:T(4,128)} %copy.119), channel_id=1, source_target_pairs={{0,32},{32,64},{64,96},{96,0},{1,33},{33,65},{65,97},{97,1},{2,34}... | collective-permute-start | bytes 61448 | tf_op jit(solution)/shard_map/ppermute | solution.py:19
  29.7 19.2 %collective-permute-start.1 = (f32[20,64,4]{1,2,0:T(4,128)}, f32[20,64,4]{1,2,0:T(4,128)}, u32[]{:S(2)}, u32[]{:S(2)}) collective-permute-start(f32[20,64,4]{1,2,0:T(4,128)} %copy.120), channel_id=1, source_target_pairs={{0,96},{32,0},{64,32},{96,64},{1,97},{33,1},{65,33},{97,65},{2,98}... | collective-permute-start | bytes 61448 | tf_op jit(solution)/shard_map/ppermute | solution.py:19
  34.5 9.1 %copy-start.23 = (s32[256]{0:T(256)}, s32[256]{0:T(256)S(1)}, u32[]{:S(2)}) copy-start(s32[256]{0:T(256)S(1)} %multiply_add_fusion.2) | copy-start | bytes 3076
  50.9 6.1 %copy-start.2 = (f32[20,64,4]{2,1,0:T(8,128)S(1)}, f32[20,64,4]{2,1,0:T(8,128)}, u32[]{:S(2)}) copy-start(f32[20,64,4]{2,1,0:T(8,128)} %copy.121) | copy-start | bytes 61444
  50.9 10.2 %copy-start.3 = (f32[20,64,4]{2,1,0:T(8,128)S(1)}, f32[20,64,4]{2,1,0:T(8,128)}, u32[]{:S(2)}) copy-start(f32[20,64,4]{2,1,0:T(8,128)} %copy.122) | copy-start | bytes 61444
  52.2 5.1 %collective-permute-start.2 = (f32[20,4,264]{2,1,0:T(4,128)S(1)}, f32[20,4,264]{2,1,0:T(4,128)S(1)}, u32[]{:S(2)}, u32[]{:S(2)}) collective-permute-start(f32[20,4,264]{2,1,0:T(4,128)S(1)} %get-tuple-element.71), channel_id=1, source_target_pairs={{0,1},{1,2},{2,3},{3,4},{4,5},{5,6},{6,7},{7,8},{8,9},{9,10},{10,1... | collective-permute-start | bytes 253448 | tf_op jit(solution)/shard_map/ppermute | solution.py:14
  55.4 5.6 %collective-permute-start.3 = (f32[20,4,264]{2,1,0:T(4,128)S(1)}, f32[20,4,264]{2,1,0:T(4,128)S(1)}, u32[]{:S(2)}, u32[]{:S(2)}) collective-permute-start(f32[20,4,264]{2,1,0:T(4,128)S(1)} %get-tuple-element.72), channel_id=1, source_target_pairs={{1,0},{2,1},{3,2},{4,3},{5,4},{6,5},{7,6},{8,7},{9,8},{10,9},{11,1... | collective-permute-start | bytes 253448 | tf_op jit(solution)/shard_map/ppermute | solution.py:14
  57.1 14.3 %copy-start.10 = (f32[4,64,256]{2,1,0:T(8,128)}, f32[4,64,256]{2,1,0:T(8,128)S(1)}, u32[]{:S(2)}) copy-start(f32[4,64,256]{2,1,0:T(8,128)S(1)} %get-tuple-element.67) | copy-start | bytes 786436
  85.2 165.2 %all-to-all-start = ((f32[128,8,128]{2,1,0:T(8,128)}), f32[128,8,128]{2,1,0:T(8,128)}, u32[]{:S(2)}, u32[]{:S(2)}) async-start(f32[128,8,128]{2,1,0:T(8,128)} %bitcast_select_fusion), calls=%async_computation | async-start | bytes 1048576 | tf_op jit(solution)/shard_map/all_to_all | solution.py:169
  107.0 142.3 %copy-start.4 = (f32[2,4,64,256]{3,2,1,0:T(8,128)}, f32[2,4,64,256]{3,2,1,0:T(8,128)S(1)}, u32[]{:S(2)}) copy-start(f32[2,4,64,256]{3,2,1,0:T(8,128)S(1)} %pad_subtract_fusion.3) | copy-start | bytes 1572868
  250.4 3.1 %copy-start.21 = (s32[64,256]{1,0:T(8,128)S(1)}, s32[64,256]{1,0:T(8,128)}, u32[]{:S(2)}) copy-start(s32[64,256]{1,0:T(8,128)} %param.21) | copy-start | bytes 196612
  254.6 11.0 %copy-start.24 = (s32[256]{0:T(256)S(1)}, s32[256]{0:T(256)}, u32[]{:S(2)}) copy-start(s32[256]{0:T(256)} %copy-done.23) | copy-start | bytes 3076
  255.4 10.4 %copy-start.20 = (s32[128,2,2]{2,1,0:T(2,128)S(1)}, s32[128,2,2]{2,1,0:T(2,128)}, u32[]{:S(2)}) copy-start(s32[128,2,2]{2,1,0:T(2,128)} %iota_add_fusion.1) | copy-start | bytes 6148
  255.4 30.1 %copy-start.35 = (pred[1024]{0:T(1024)(128)(4,1)S(1)}, pred[1024]{0:T(1024)(128)(4,1)}, u32[]{:S(2)}) copy-start(pred[1024]{0:T(1024)(128)(4,1)} %fusion.121) | copy-start | bytes 3076
  257.0 28.5 %all-to-all-start.1 = ((f32[128,8,128]{2,1,0:T(8,128)}), f32[128,8,128]{2,1,0:T(8,128)S(1)}, u32[]{:S(2)}, u32[]{:S(2)}) async-start(f32[128,8,128]{2,1,0:T(8,128)} %fusion.17), calls=%async_computation.1 | async-start | bytes 1048576 | tf_op jit(solution)/shard_map/all_to_all | solution.py:214
  297.2 6.3 %collective-permute-start.5 = (f32[2,64,256]{2,1,0:T(8,128)S(1)}, f32[2,64,256]{2,1,0:T(8,128)S(1)}, u32[]{:S(2)}, u32[]{:S(2)}) collective-permute-start(f32[2,64,256]{2,1,0:T(8,128)S(1)} %reshape.713), channel_id=1, source_target_pairs={{128,0},{129,1},{130,2},{131,3},{132,4},{133,5},{134,6},{135,7},{1... | collective-permute-start | bytes 393224 | tf_op jit(solution)/shard_map/ppermute | solution.py:14
  (21 other events, 37.1 us)
Sparse Core Ops, SparseCore 0:
  11.6 225.6 all-gather.1
